TPU v7x, 32 devices: a whole 2x2x4 slice. The times are simulated.
32 devices in a mesh: section: 2 (over core), dp: 4 (over y, x), ctx: 4 (over z).
Axes of the slice: x: 2, y: 2, z: 4, core: 2. Of those that a mesh axis runs over, the one named last changes fastest.
Arguments:
- tokens: bfloat16 [2, 8, 1024, 768], P(None, 'dp', 'ctx'), may hold values from -6 to 6
- upstream: bfloat16 [2, 8, 1024, 768], P(None, 'dp', 'ctx'), may hold values from -6 to 6
- lengths: int32 [2, 8], P(None, 'dp'), may hold values from 512 to 1024, as said below
- w_qkv: float32 [2, 768, 2304], P('section', ('dp', 'ctx')), may hold values from -0.21875 to 0.21875
- w_out: float32 [2, 768, 768], P('section', ('dp', 'ctx')), may hold values from -4 to 4
- w_in: float32 [2, 768, 3072], P('section', ('dp', 'ctx')), may hold values from -0.21875 to 0.21875
- w_back: float32 [2, 3072, 768], P('section', ('dp', 'ctx')), may hold values from -0.109375 to 0.109375
- gain_attn: float32 [2, 768], P('section', ('dp', 'ctx')), may hold values from 0.1 to 1.9
- gain_ffn: float32 [2, 768], P('section', ('dp', 'ctx')), may hold values from 0.1 to 1.9
Outputs:
- acts: float32 [2, 2, 8, 1024, 768], P('section', None, 'dp', 'ctx')
- grads: float32 [2, 2, 8, 1024, 768], P('section', None, 'dp', 'ctx')
- grad_qkv: float32 [2, 768, 2304], P('section', ('dp', 'ctx'))
- grad_out: float32 [2, 768, 768], P('section', ('dp', 'ctx'))
- grad_in: float32 [2, 768, 3072], P('section', ('dp', 'ctx'))
- grad_back: float32 [2, 3072, 768], P('section', ('dp', 'ctx'))
- grad_gain_attn: float32 [2, 768], P('section', ('dp', 'ctx'))
- grad_gain_ffn: float32 [2, 768], P('section', ('dp', 'ctx'))
Inputs may be any that keep to these rules, and one draw needn't show every extreme that they name: `lengths`: the number of real codons of each sequence, from 512 to 1024; some sequence has exactly 1024 and some exactly 512.
All inputs are finite; a program needn't handle non-finite values.
Results may differ from a plain program's by a relative error of at most 0.038.
Values may be sent and summed in bfloat16 or wider, within the bound.
No kernel may reach another device: no remote copies, remote signals or barrier semaphores. Data moves between devices by JAX's collectives and lax.ppermute only.
A program may use at most 320 MiB of HBM per device.

v0:
```python
from functools import partial
import jax
import jax.numpy as jnp
from jax import lax
from jax.sharding import PartitionSpec as P

HD = 64


def passed_along(value, axis, steps):
    count = lax.axis_size(axis)
    leading, last = (max(0, -steps), min(count, count - steps))
    return lax.ppermute(value, axis, [(source, source + steps) for source in range(leading, last)])


def tables(positions):
    half_width = HD // 2
    frequency = jnp.power(10000.0, -(jnp.arange(half_width).astype(jnp.float32) * 2.0) / HD)
    angles = positions[:, None] * frequency[None, :]
    angles = jnp.concatenate([angles, angles], axis=1)
    return (jnp.cos(angles)[:, None, :], jnp.sin(angles)[:, None, :])


def rotate(tensor, cosine_tab, sine_tab):
    half_width = tensor.shape[-1] // 2
    turned = jnp.concatenate([-tensor[..., half_width:], tensor[..., :half_width]], axis=-1)
    return tensor * cosine_tab + turned * sine_tab


def layer_norm(residual_state, gain_vec):
    centred = residual_state - jnp.mean(residual_state, axis=-1, keepdims=True)
    spread = jnp.mean(centred * centred, axis=-1, keepdims=True)
    return centred * lax.rsqrt(spread + 1e-05) * gain_vec


def contract_rows(left_op, right_op):
    return lax.dot_general(
        left_op, right_op, (((0,), (0,)), ((), ())), preferred_element_type=jnp.float32
    )


def contract_cols(left_op, right_op):
    return lax.dot_general(
        left_op, right_op, (((1,), (1,)), ((), ())), preferred_element_type=jnp.float32
    )


def store(buffer, new_value, position, in_range):
    previous = lax.dynamic_index_in_dim(buffer, position, 0, keepdims=False)
    return lax.dynamic_update_index_in_dim(
        buffer, jnp.where(in_range, new_value, previous), position, 0
    )


def split_heads(tensor):
    return tensor.reshape(tensor.shape[0], tensor.shape[1], tensor.shape[2] // HD, HD)


def masked_scores(query, key_all, key_mask):
    scores = jnp.einsum(
        "sqhd,skhd->shqk",
        split_heads(query),
        split_heads(key_all),
        preferred_element_type=jnp.float32,
    )
    return jnp.where(key_mask[:, None, None, :], scores, -1e30)


def attention_forward(query, key_all, value_all, key_mask):
    scores = masked_scores(query, key_all, key_mask)
    row_peak = jnp.max(scores, axis=-1, keepdims=True)
    log_total = row_peak + jnp.log(jnp.sum(jnp.exp(scores - row_peak), axis=-1, keepdims=True))
    probabilities = jnp.exp(scores - log_total).astype(jnp.bfloat16)
    attended_output = jnp.einsum(
        "shqk,skhd->sqhd", probabilities, split_heads(value_all), preferred_element_type=jnp.float32
    )
    return (attended_output.reshape(query.shape).astype(jnp.bfloat16), log_total)


def attention_backward(query, key_all, value_all, key_mask, log_total, grad_attended):
    scores = masked_scores(query, key_all, key_mask)
    probabilities = jnp.exp(scores - log_total)
    low_probs = probabilities.astype(jnp.bfloat16)
    grad_heads = split_heads(grad_attended)
    grad_probs = jnp.einsum(
        "sqhd,skhd->shqk", grad_heads, split_heads(value_all), preferred_element_type=jnp.float32
    )
    delta = jnp.sum(probabilities * grad_probs, axis=-1, keepdims=True)
    grad_scores = (probabilities * (grad_probs - delta)).astype(jnp.bfloat16)
    grad_query = jnp.einsum(
        "shqk,skhd->sqhd", grad_scores, split_heads(key_all), preferred_element_type=jnp.float32
    )
    grad_keys = jnp.einsum(
        "shqk,sqhd->skhd", grad_scores, split_heads(query), preferred_element_type=jnp.float32
    )
    grad_values = jnp.einsum(
        "shqk,sqhd->skhd", low_probs, grad_heads, preferred_element_type=jnp.float32
    )
    return (
        grad_query.reshape(query.shape),
        grad_keys.reshape(key_all.shape),
        grad_values.reshape(key_all.shape),
    )


def local(tokens, upstream, lengths, w_qkv, w_out, w_in, w_back, gain_attn, gain_ffn):
    section_count = lax.axis_size("section")
    section_index = lax.axis_index("section")
    micro_count, sequences, span_rows, model_width = tokens.shape
    head_count = model_width // HD
    key_count = span_rows * lax.axis_size("ctx")
    ctx_index = lax.axis_index("ctx")
    q_scale = HD ** (-0.5)
    qkv_low = w_qkv[0].astype(jnp.bfloat16)
    out_low = w_out[0].astype(jnp.bfloat16)
    in_low = w_in[0].astype(jnp.bfloat16)
    back_low = w_back[0].astype(jnp.bfloat16)
    attn_low = gain_attn[0].astype(jnp.bfloat16)
    ffn_low = gain_ffn[0].astype(jnp.bfloat16)
    (
        query_key_value_matrix,
        output_weight_matrix,
        input_weight_matrix,
        back_weight_matrix,
        gain_one,
        gain_two,
    ) = (
        lax.all_gather(qkv_low, ("dp", "ctx"), axis=0, tiled=True),
        lax.all_gather(out_low, ("dp", "ctx"), axis=0, tiled=True),
        lax.all_gather(in_low, ("dp", "ctx"), axis=0, tiled=True),
        lax.all_gather(back_low, ("dp", "ctx"), axis=0, tiled=True),
        lax.all_gather(attn_low, ("dp", "ctx"), axis=0, tiled=True),
        lax.all_gather(ffn_low, ("dp", "ctx"), axis=0, tiled=True),
    )
    gain_one = gain_one.astype(jnp.float32)
    gain_two = gain_two.astype(jnp.float32)
    positions = (ctx_index * span_rows + jnp.arange(span_rows)).astype(jnp.float32)
    cosine_tab, sine_tab = tables(positions)
    key_places = jnp.arange(key_count)
    row_total = sequences * span_rows
    span_shape = (sequences, span_rows, model_width)

    def scaled_rotate(tensor):
        return rotate(tensor, cosine_tab, sine_tab) * q_scale

    def plain_rotate(tensor):
        return rotate(tensor, cosine_tab, sine_tab)

    def mask_for(which_batch):
        lengths_now = lax.dynamic_index_in_dim(lengths, which_batch, 0, keepdims=False)
        return key_places[None, :] < lengths_now[:, None]

    moments = micro_count + section_count - 1
    acts = jnp.zeros((micro_count,) + span_shape, jnp.float32)
    inbound = jnp.zeros(span_shape, jnp.float32)
    stored = None
    for moment in range(moments):
        micro_index = moment - section_index
        in_range = (micro_index >= 0) & (micro_index < micro_count)
        which_batch = jnp.clip(micro_index, 0, micro_count - 1)
        fresh = lax.dynamic_index_in_dim(tokens, which_batch, 0, keepdims=False).astype(jnp.float32)
        source = jnp.where(section_index == 0, fresh, inbound)
        forward_residual_in = source.reshape(row_total, model_width)
        forward_normed_input = layer_norm(forward_residual_in, gain_one).astype(jnp.bfloat16)
        query_key_value_rows = jnp.dot(
            forward_normed_input, query_key_value_matrix, preferred_element_type=jnp.float32
        )
        query_key_value_rows = query_key_value_rows.reshape(sequences, span_rows, 3, head_count, HD)
        forward_query = (
            scaled_rotate(query_key_value_rows[:, :, 0]).astype(jnp.bfloat16).reshape(span_shape)
        )
        forward_key_rows = (
            plain_rotate(query_key_value_rows[:, :, 1]).astype(jnp.bfloat16).reshape(span_shape)
        )
        forward_value_rows = query_key_value_rows[:, :, 2].astype(jnp.bfloat16).reshape(span_shape)
        forward_key_all = lax.all_gather(forward_key_rows, "ctx", axis=1, tiled=True)
        forward_value_all = lax.all_gather(forward_value_rows, "ctx", axis=1, tiled=True)
        forward_attended_output, forward_log_total = attention_forward(
            forward_query, forward_key_all, forward_value_all, mask_for(which_batch)
        )
        forward_middle_state = forward_residual_in + jnp.dot(
            forward_attended_output.reshape(row_total, model_width),
            output_weight_matrix,
            preferred_element_type=jnp.float32,
        )
        forward_normed_second = layer_norm(forward_middle_state, gain_two).astype(jnp.bfloat16)
        forward_hidden_before_gelu = jnp.dot(
            forward_normed_second, input_weight_matrix, preferred_element_type=jnp.float32
        )
        forward_hidden_activation = jax.nn.gelu(
            forward_hidden_before_gelu, approximate=False
        ).astype(jnp.bfloat16)
        result = forward_middle_state + jnp.dot(
            forward_hidden_activation, back_weight_matrix, preferred_element_type=jnp.float32
        )
        forward_saved = (
            forward_residual_in,
            forward_query,
            forward_key_rows,
            forward_value_rows,
            forward_log_total,
            forward_attended_output,
            forward_middle_state,
            forward_hidden_before_gelu,
            forward_hidden_activation,
        )
        result, saved = (result.reshape(span_shape), forward_saved)
        if stored is None:
            stored = tuple((jnp.zeros((micro_count,) + item.shape, item.dtype) for item in saved))
        stored = tuple(
            (store(buffer, item, which_batch, in_range) for buffer, item in zip(stored, saved))
        )
        acts = store(acts, result, which_batch, in_range)
        if moment + 1 < moments:
            inbound = passed_along(result.astype(jnp.bfloat16), "section", 1).astype(result.dtype)
    grads_in = jnp.zeros((micro_count,) + span_shape, jnp.float32)
    inbound_grad = jnp.zeros(span_shape, jnp.float32)
    full_totals = (
        jnp.zeros(query_key_value_matrix.shape, jnp.float32),
        jnp.zeros(output_weight_matrix.shape, jnp.float32),
        jnp.zeros(input_weight_matrix.shape, jnp.float32),
        jnp.zeros(back_weight_matrix.shape, jnp.float32),
        jnp.zeros(gain_one.shape, jnp.float32),
        jnp.zeros(gain_two.shape, jnp.float32),
    )
    shard_totals = (
        jnp.zeros_like(w_qkv[0]),
        jnp.zeros_like(w_out[0]),
        jnp.zeros_like(w_in[0]),
        jnp.zeros_like(w_back[0]),
        jnp.zeros_like(gain_attn[0]),
        jnp.zeros_like(gain_ffn[0]),
    )
    for moment in range(moments):
        micro_index = moment - (section_count - 1 - section_index)
        in_range = (micro_index >= 0) & (micro_index < micro_count)
        which_batch = jnp.clip(micro_index, 0, micro_count - 1)
        fresh = lax.dynamic_index_in_dim(upstream, which_batch, 0, keepdims=False).astype(
            jnp.float32
        )
        incoming = jnp.where(section_index == section_count - 1, fresh, inbound_grad)
        saved = tuple(
            (lax.dynamic_index_in_dim(buffer, which_batch, 0, keepdims=False) for buffer in stored)
        )
        (
            residual_in,
            query,
            key_rows,
            value_rows,
            log_total,
            attended_output,
            middle_state,
            hidden_before_gelu,
            hidden_activation,
        ) = saved[:9]
        grad_top = incoming.reshape(row_total, model_width)
        low_top = grad_top.astype(jnp.bfloat16)
        grad_w_back = contract_rows(hidden_activation, low_top)
        grad_hidden = contract_cols(low_top, back_weight_matrix)
        gelu_primal, gelu_back = jax.vjp(
            partial(jax.nn.gelu, approximate=False), hidden_before_gelu
        )
        grad_pre = gelu_back(grad_hidden)[0].astype(jnp.bfloat16)
        normed_second, norm_two_back = jax.vjp(layer_norm, middle_state, gain_two)
        grad_w_in = contract_rows(normed_second.astype(jnp.bfloat16), grad_pre)
        grad_normed_two = contract_cols(grad_pre, input_weight_matrix)
        grad_mid_norm, grad_gain_two = norm_two_back(grad_normed_two)
        grad_middle = grad_top + grad_mid_norm
        low_middle = grad_middle.astype(jnp.bfloat16)
        grad_w_out = contract_rows(attended_output.reshape(row_total, model_width), low_middle)
        grad_attended = (
            contract_cols(low_middle, output_weight_matrix).astype(jnp.bfloat16).reshape(span_shape)
        )
        key_all = lax.all_gather(key_rows, "ctx", axis=1, tiled=True)
        value_all = lax.all_gather(value_rows, "ctx", axis=1, tiled=True)
        grad_query, grad_keys, grad_values = attention_backward(
            query, key_all, value_all, mask_for(which_batch), log_total, grad_attended
        )
        grad_keys, grad_values = (
            lax.psum_scatter(
                grad_keys.astype(jnp.bfloat16), "ctx", scatter_dimension=1, tiled=True
            ).astype(jnp.float32),
            lax.psum_scatter(
                grad_values.astype(jnp.bfloat16), "ctx", scatter_dimension=1, tiled=True
            ).astype(jnp.float32),
        )
        heads_shape = (sequences, span_rows, head_count, HD)
        zero_heads = jnp.zeros(heads_shape, jnp.float32)
        rotated_q, q_back = jax.vjp(scaled_rotate, zero_heads)
        rotated_k, k_back = jax.vjp(plain_rotate, zero_heads)
        low_query = grad_query.astype(jnp.bfloat16).astype(jnp.float32).reshape(heads_shape)
        low_keys = grad_keys.astype(jnp.bfloat16).astype(jnp.float32).reshape(heads_shape)
        part_q = q_back(low_query)[0]
        part_k = k_back(low_keys)[0]
        part_v = grad_values.reshape(heads_shape)
        grad_qkv = (
            jnp.stack([part_q, part_k, part_v], axis=2)
            .reshape(row_total, 3 * model_width)
            .astype(jnp.bfloat16)
        )
        normed_input, norm_one_back = jax.vjp(layer_norm, residual_in, gain_one)
        grad_w_qkv = contract_rows(normed_input.astype(jnp.bfloat16), grad_qkv)
        grad_normed = contract_cols(grad_qkv, query_key_value_matrix)
        grad_in_norm, grad_gain_one = norm_one_back(grad_normed)
        grad_source = grad_middle + grad_in_norm
        partial_grads = (
            grad_w_qkv,
            grad_w_out,
            grad_w_in,
            grad_w_back,
            grad_gain_one,
            grad_gain_two,
        )
        grad_source, partial_grads = (grad_source.reshape(span_shape), partial_grads)
        g_qkv, g_out, g_in, g_back, g_one, g_two = tuple(
            (jnp.where(in_range, item, 0.0) for item in partial_grads)
        )
        grads_in = store(grads_in, grad_source, which_batch, in_range)
        full_totals = tuple(
            (
                total + item
                for total, item in zip(full_totals, (g_qkv, g_out, g_in, g_back, g_one, g_two))
            )
        )
        if moment + 1 < moments:
            inbound_grad = passed_along(grad_source.astype(jnp.bfloat16), "section", -1).astype(
                grad_source.dtype
            )
    sum_qkv, sum_out, sum_in, sum_back, sum_one, sum_two = full_totals
    shard_totals = (
        lax.psum_scatter(sum_qkv, ("dp", "ctx"), scatter_dimension=0, tiled=True),
        lax.psum_scatter(sum_out, ("dp", "ctx"), scatter_dimension=0, tiled=True),
        lax.psum_scatter(sum_in, ("dp", "ctx"), scatter_dimension=0, tiled=True),
        lax.psum_scatter(sum_back, ("dp", "ctx"), scatter_dimension=0, tiled=True),
        lax.psum_scatter(sum_one, ("dp", "ctx"), scatter_dimension=0, tiled=True),
        lax.psum_scatter(sum_two, ("dp", "ctx"), scatter_dimension=0, tiled=True),
    )
    return (
        acts[None],
        grads_in[None],
        shard_totals[0][None],
        shard_totals[1][None],
        shard_totals[2][None],
        shard_totals[3][None],
        shard_totals[4][None],
        shard_totals[5][None],
    )


def solution(mesh):
    return jax.shard_map(
        local,
        mesh=mesh,
        in_specs=(
            P(None, "dp", "ctx", None),
            P(None, "dp", "ctx", None),
            P(None, "dp"),
            P("section", ("dp", "ctx"), None),
            P("section", ("dp", "ctx"), None),
            P("section", ("dp", "ctx"), None),
            P("section", ("dp", "ctx"), None),
            P("section", ("dp", "ctx")),
            P("section", ("dp", "ctx")),
        ),
        out_specs=(
            P("section", None, "dp", "ctx", None),
            P("section", None, "dp", "ctx", None),
            P("section", ("dp", "ctx"), None),
            P("section", ("dp", "ctx"), None),
            P("section", ("dp", "ctx"), None),
            P("section", ("dp", "ctx"), None),
            P("section", ("dp", "ctx")),
            P("section", ("dp", "ctx")),
        ),
        check_vma=False,
    )
```

profile of v0, /device:TPU:0, one launch (start us, length us, event | category | flops | bytes accessed | tf_op | source)
XLA Modules:
  0.0 2275.4 jit_solution(7702583870397529192)
XLA Ops:
  12.7 44.1 %all-reduce.17 = (bf16[768]{0:T(1024)(128)(2,1)S(1)}, bf16[768]{0:T(1024)(128)(2,1)S(1)}) all-reduce(bf16[768]{0:T(1024)(128)(2,1)S(1)} %dynamic-update-slice, bf16[768]{0:T(1024)(128)(2,1)S(1)} %dynamic-update-slice.1), channel_id=2, replica_groups=mesh['section'=2,'dp'=4,'ctx'=4] {'dp','ctx'}, use_global_device_ids=true, to_apply=%add.12 | all-reduce | flops 1536 | bytes 6144
  62.2 23.0 %all-gather.41.cloned.1.call-done = bf16[1,768,2304]{2,1,0:T(8,128)(2,1)} async-done(((bf16[1,48,2304]{2,1,0:T(8,128)(2,1)}), bf16[1,768,2304]{2,1,0:T(8,128)(2,1)}) %all-gather.41.cloned.1.call-update) | async-done | bytes 3538960 | tf_op jit(solution)/shard_map/all_gather | solution.py:128
  85.3 5.9 copy.104
  109.0 54.5 %all-gather.31.cloned.1.call-done = bf16[2,1024,768]{1,2,0:T(8,128)(2,1)} async-done(((bf16[2,256,768]{1,2,0:T(8,128)(2,1)}), bf16[2,1024,768]{1,2,0:T(8,128)(2,1)}) %all-gather.31.cloned.1.call-update) | async-done | bytes 3145744 | tf_op jit(solution)/shard_map/all_gather | solution.py:176
  163.5 14.9 select_reduce_fusion.2
  178.4 11.1 exponential_reduce_fusion.2
  189.6 37.1 %all-gather.29.cloned.1.call-done = bf16[2,1024,768]{1,2,0:T(8,128)(2,1)} async-done(((bf16[2,256,768]{1,2,0:T(8,128)(2,1)}), bf16[2,1024,768]{1,2,0:T(8,128)(2,1)}) %all-gather.29.cloned.1.call-update) | async-done | bytes 3145744 | tf_op jit(solution)/shard_map/all_gather | solution.py:177
  226.7 12.5 broadcast_select_fusion.2
  241.1 43.2 %all-gather.43.cloned.1.call-done = bf16[1,768,768]{2,1,0:T(8,128)(2,1)} async-done(((bf16[1,48,768]{2,1,0:T(8,128)(2,1)}), bf16[1,768,768]{2,1,0:T(8,128)(2,1)}) %all-gather.43.cloned.1.call-update) | async-done | bytes 1179664 | tf_op jit(solution)/shard_map/all_gather | solution.py:129
  287.5 79.3 %all-gather.45.cloned.1.call-done = bf16[1,768,3072]{2,1,0:T(8,128)(2,1)} async-done(((bf16[1,48,3072]{2,1,0:T(8,128)(2,1)}), bf16[1,768,3072]{2,1,0:T(8,128)(2,1)}) %all-gather.45.cloned.1.call-update) | async-done | bytes 4718608 | tf_op jit(solution)/shard_map/all_gather | solution.py:130
  370.7 21.0 bitcast_dynamic-update-slice_fusion.5
  391.7 57.5 %all-gather.47.cloned.1.call-done = bf16[1,3072,768]{2,1,0:T(8,128)(2,1)} async-done(((bf16[1,192,768]{2,1,0:T(8,128)(2,1)}), bf16[1,3072,768]{2,1,0:T(8,128)(2,1)}) %all-gather.47.cloned.1.call-update) | async-done | bytes 4718608 | tf_op jit(solution)/shard_map/all_gather | solution.py:131
  449.1 7.2 fusion.397
  476.4 54.9 %all-gather.35.cloned.1.call-done = bf16[2,1024,768]{1,2,0:T(8,128)(2,1)} async-done(((bf16[2,256,768]{1,2,0:T(8,128)(2,1)}), bf16[2,1024,768]{1,2,0:T(8,128)(2,1)}) %all-gather.35.cloned.1.call-update) | async-done | bytes 3145744 | tf_op jit(solution)/shard_map/all_gather | solution.py:176
  531.3 15.3 select_reduce_fusion.1
  546.5 11.3 exponential_reduce_fusion.1
  557.9 36.5 %all-gather.33.cloned.1.call-done = bf16[2,1024,768]{1,2,0:T(8,128)(2,1)} async-done(((bf16[2,256,768]{1,2,0:T(8,128)(2,1)}), bf16[2,1024,768]{1,2,0:T(8,128)(2,1)}) %all-gather.33.cloned.1.call-update) | async-done | bytes 3145744 | tf_op jit(solution)/shard_map/all_gather | solution.py:177
  594.5 11.6 fusion.215
  609.6 20.3 bitcast_dynamic-update-slice_fusion.4
  736.7 6.2 bitcast_dynamic-update-slice_fusion.1
  754.5 14.9 select_reduce_fusion
  769.3 11.6 exponential_reduce_fusion
  781.0 11.8 fusion.214
  802.0 20.0 bitcast_dynamic-update-slice_fusion.3
  826.7 18.8 fusion.43
  857.5 12.2 fusion.403
  869.7 29.4 %all-gather.51.cloned.1.call-done = bf16[1,2,1024,768]{3,2,1,0:T(8,128)(2,1)} async-done(((bf16[1,2,256,768]{3,2,1,0:T(8,128)(2,1)}), bf16[1,2,1024,768]{3,2,1,0:T(8,128)(2,1)}) %all-gather.51.cloned.1.call-update) | async-done | bytes 3145744 | tf_op jit(solution)/shard_map/all_gather | solution.py:275
  902.4 17.2 multiply_reduce_fusion.2
  919.6 16.9 multiply_convert_fusion.2
  943.1 12.3 fusion.170
  959.5 9.5 bitcast_multiply_fusion.13
  975.7 50.8 %all-gather.55.cloned.1.call-done = bf16[1,2,1024,768]{3,2,1,0:T(8,128)(2,1)} async-done(((bf16[1,2,256,768]{3,2,1,0:T(8,128)(2,1)}), bf16[1,2,1024,768]{3,2,1,0:T(8,128)(2,1)}) %all-gather.55.cloned.1.call-update) | async-done | bytes 3145744 | tf_op jit(solution)/shard_map/all_gather | solution.py:275
  1031.2 56.5 %reduce-scatter.11.cloned.1.call-done = bf16[2,256,768]{1,2,0:T(8,128)(2,1)} async-done(((bf16[2,1024,768]{1,2,0:T(8,128)(2,1)}), bf16[2,256,768]{1,2,0:T(8,128)(2,1)}) %reduce-scatter.11.cloned.1.call-update) | async-done | bytes 786448 | tf_op jit(solution)/shard_map/reduce_scatter | solution.py:280
  1090.5 59.7 %reduce-scatter.13.cloned.1.call-done = bf16[2,256,768]{1,2,0:T(8,128)(2,1)} async-done(((bf16[2,1024,768]{1,2,0:T(8,128)(2,1)}), bf16[2,256,768]{1,2,0:T(8,128)(2,1)}) %reduce-scatter.13.cloned.1.call-update) | async-done | bytes 786448 | tf_op jit(solution)/shard_map/reduce_scatter | solution.py:283
  1165.2 11.1 fusion.404
  1177.6 17.8 fusion.48
  1202.3 17.9 multiply_reduce_fusion.1
  1220.1 17.5 multiply_convert_fusion.1
  1243.1 12.3 fusion.173
  1261.4 17.3 all-gather.59.cloned.1.call-done
  1283.4 10.1 bitcast_multiply_fusion.11
  1295.5 44.4 %reduce-scatter.15.cloned.1.call-done = bf16[2,256,768]{1,2,0:T(8,128)(2,1)} async-done(((bf16[2,1024,768]{1,2,0:T(8,128)(2,1)}), bf16[2,256,768]{1,2,0:T(8,128)(2,1)}) %reduce-scatter.15.cloned.1.call-update) | async-done | bytes 786448 | tf_op jit(solution)/shard_map/reduce_scatter | solution.py:280
  1342.8 59.6 %reduce-scatter.17.cloned.1.call-done = bf16[2,256,768]{1,2,0:T(8,128)(2,1)} async-done(((bf16[2,1024,768]{1,2,0:T(8,128)(2,1)}), bf16[2,256,768]{1,2,0:T(8,128)(2,1)}) %reduce-scatter.17.cloned.1.call-update) | async-done | bytes 786448 | tf_op jit(solution)/shard_map/reduce_scatter | solution.py:283
  1416.7 11.0 fusion.405
  1429.0 18.0 fusion.53
  1459.6 18.2 multiply_reduce_fusion
  1477.8 16.7 multiply_convert_fusion
  1500.1 13.0 fusion.176
  1535.3 4.9 fusion.263
  1540.2 5.4 fusion.264
  1545.6 8.9 select_add_fusion.1
  1555.6 4.7 fusion.165
  1560.4 4.8 fusion.163
  1565.2 9.1 select_add_fusion
  1576.2 7.1 fusion.256
  1583.3 5.2 fusion.259
  1588.5 8.6 bitcast_multiply_fusion.9
  1601.9 22.6 reduce-scatter.21.cloned.1.call-done
  1630.9 8.6 select_add_fusion.2
  1659.9 42.1 %all-reduce.16 = (f32[768]{0:T(1024)S(1)}, f32[768]{0:T(1024)S(1)}) all-reduce(f32[768]{0:T(1024)S(1)} %select_add_fusion.5, f32[768]{0:T(1024)S(1)} %select_add_fusion.4), channel_id=24, replica_groups=mesh['section'=2,'dp'=4,'ctx'=4] {'dp','ctx'}, use_global_device_ids=true, to_apply=%region_58.59.clone | all-reduce | flops 1536 | bytes 12288
  1708.4 49.4 %reduce-scatter.25.cloned.1.call-done = f32[48,768]{1,0:T(8,128)} async-done(((f32[768,768]{1,0:T(8,128)}), f32[48,768]{1,0:T(8,128)}) %reduce-scatter.25.cloned.1.call-update) | async-done | bytes 147472 | tf_op jit(solution)/shard_map/reduce_scatter | solution.py:332
  1757.8 177.4 %reduce-scatter.27.cloned.1.call-done = f32[48,3072]{1,0:T(8,128)} async-done(((f32[768,3072]{1,0:T(8,128)}), f32[48,3072]{1,0:T(8,128)}) %reduce-scatter.27.cloned.1.call-update) | async-done | bytes 589840 | tf_op jit(solution)/shard_map/reduce_scatter | solution.py:333
  1935.2 176.4 %reduce-scatter.29.cloned.1.call-done = f32[192,768]{1,0:T(8,128)} async-done(((f32[3072,768]{1,0:T(8,128)}), f32[192,768]{1,0:T(8,128)}) %reduce-scatter.29.cloned.1.call-update) | async-done | bytes 589840 | tf_op jit(solution)/shard_map/reduce_scatter | solution.py:334
  2111.6 156.8 %reduce-scatter.23.cloned.1.call-done = f32[48,2304]{1,0:T(8,128)} async-done(((f32[768,2304]{1,0:T(8,128)}), f32[48,2304]{1,0:T(8,128)}) %reduce-scatter.23.cloned.1.call-update) | async-done | bytes 442384 | tf_op jit(solution)/shard_map/reduce_scatter | solution.py:331
  (757 shorter events, 370.7 us)
Async XLA Ops:
  7.2 78.1 %all-gather.41.cloned.1.call-start = ((), (), s32[]{:S(2)}) async-start(), calls=%async_computation.26 | async-start | bytes 3760128 | tf_op jit(solution)/shard_map/all_gather | solution.py:128
  9.0 154.6 %all-gather.31.cloned.1.call-start = ((), (), s32[]{:S(2)}) async-start(), calls=%async_computation.11 | async-start | bytes 3932160 | tf_op jit(solution)/shard_map/all_gather | solution.py:176
  56.8 581.6 %copy-start.139 = (f32[768]{0:T(1024)}, f32[768]{0:T(1024)S(1)}, u32[]{:S(2)}) copy-start(f32[768]{0:T(1024)S(1)} %convert_element_type.771) | copy-start | bytes 9220
  59.1 472.2 %copy-start.64 = (f32[256,64]{0,1:T(8,128)}, f32[256,64]{0,1:T(8,128)S(1)}, u32[]{:S(2)}) copy-start(f32[256,64]{0,1:T(8,128)S(1)} %get-tuple-element.135) | copy-start | bytes 196612
  59.1 472.2 %copy-start.69 = (f32[256,64]{0,1:T(8,128)}, f32[256,64]{0,1:T(8,128)S(1)}, u32[]{:S(2)}) copy-start(f32[256,64]{0,1:T(8,128)S(1)} %get-tuple-element.134) | copy-start | bytes 196612
  101.4 125.3 %all-gather.29.cloned.1.call-start = ((), (), s32[]{:S(2)}) async-start(), calls=%async_computation.10 | async-start | bytes 3932160 | tf_op jit(solution)/shard_map/all_gather | solution.py:177
  104.2 180.1 %all-gather.43.cloned.1.call-start = ((), (), s32[]{:S(2)}) async-start(), calls=%async_computation.27 | async-start | bytes 1253376 | tf_op jit(solution)/shard_map/all_gather | solution.py:129
  105.0 261.9 %all-gather.45.cloned.1.call-start = ((), (), s32[]{:S(2)}) async-start(), calls=%async_computation.28 | async-start | bytes 5013504 | tf_op jit(solution)/shard_map/all_gather | solution.py:130
  105.8 343.3 %all-gather.47.cloned.1.call-start = ((), (), s32[]{:S(2)}) async-start(), calls=%async_computation.29 | async-start | bytes 5013504 | tf_op jit(solution)/shard_map/all_gather | solution.py:131
  106.6 424.7 %all-gather.35.cloned.1.call-start = ((), (), s32[]{:S(2)}) async-start(), calls=%async_computation.13 | async-start | bytes 3932160 | tf_op jit(solution)/shard_map/all_gather | solution.py:176
  107.4 741.9 %copy-start.126 = (f32[768]{0:T(1024)}, f32[768]{0:T(1024)S(1)}, u32[]{:S(2)}) copy-start(f32[768]{0:T(1024)S(1)} %convert_element_type.772) | copy-start | bytes 9220
  109.0 69.4 %copy-start.76 = (f32[2,256,12,32]{1,3,2,0:T(8,128)}, f32[2,256,12,32]{1,3,2,0:T(8,128)S(1)}, u32[]{:S(2)}) copy-start(f32[2,256,12,32]{1,3,2,0:T(8,128)S(1)} %get-tuple-element.125) | copy-start | bytes 2359300
  109.0 69.4 %copy-start.77 = (f32[2,256,12,32]{1,3,2,0:T(8,128)}, f32[2,256,12,32]{1,3,2,0:T(8,128)S(1)}, u32[]{:S(2)}) copy-start(f32[2,256,12,32]{1,3,2,0:T(8,128)S(1)} %get-tuple-element.126) | copy-start | bytes 2359300
  287.2 161.9 %copy-start.35 = (f32[512,768]{1,0:T(8,128)}, f32[512,768]{1,0:T(8,128)S(1)}, u32[]{:S(2)}) copy-start(f32[512,768]{1,0:T(8,128)S(1)} %get-tuple-element.147) | copy-start | bytes 4718596
  456.3 3.4 collective-permute-start
  460.0 147.1 %copy-start.22 = (f32[2,256,768]{2,1,0:T(8,128)}, f32[2,256,768]{2,1,0:T(8,128)S(1)}, u32[]{:S(2)}) copy-start(f32[2,256,768]{2,1,0:T(8,128)S(1)} %get-tuple-element.69) | copy-start | bytes 4718596
  468.5 125.9 %all-gather.33.cloned.1.call-start = ((), (), s32[]{:S(2)}) async-start(), calls=%async_computation.12 | async-start | bytes 3932160 | tf_op jit(solution)/shard_map/all_gather | solution.py:177
  471.0 283.4 %all-gather.39.cloned.1.call-start = ((), (), s32[]{:S(2)}) async-start(), calls=%async_computation.15 | async-start | bytes 3932160 | tf_op jit(solution)/shard_map/all_gather | solution.py:176
  557.9 48.2 %copy-start.132 = (f32[2,2,12,256,1]{3,2,1,4,0:T(8,128)}, f32[2,2,12,256,1]{3,2,1,4,0:T(8,128)S(1)}, u32[]{:S(2)}) copy-start(f32[2,2,12,256,1]{3,2,1,4,0:T(8,128)S(1)} %get-tuple-element.60) | copy-start | bytes 147460
  607.7 22.2 slice-start.11
  608.6 21.2 copy-start.40
  609.6 20.3 slice-start.12
  633.7 4.1 collective-permute-start.1
  647.4 133.6 %all-gather.37.cloned.1.call-start = ((), (), s32[]{:S(2)}) async-start(), calls=%async_computation.14 | async-start | bytes 3932160 | tf_op jit(solution)/shard_map/all_gather | solution.py:177
  649.9 204.4 %all-gather.49.cloned.1.call-start = ((), (), s32[]{:S(2)}) async-start(), calls=%async_computation.30 | async-start | bytes 3932160 | tf_op jit(solution)/shard_map/all_gather | solution.py:274
  706.8 192.4 %all-gather.51.cloned.1.call-start = ((), (), s32[]{:S(2)}) async-start(), calls=%async_computation.31 | async-start | bytes 3932160 | tf_op jit(solution)/shard_map/all_gather | solution.py:275
  714.0 257.1 %all-gather.53.cloned.1.call-start = ((), (), s32[]{:S(2)}) async-start(), calls=%async_computation.32 | async-start | bytes 3932160 | tf_op jit(solution)/shard_map/all_gather | solution.py:274
  719.9 306.6 %all-gather.55.cloned.1.call-start = ((), (), s32[]{:S(2)}) async-start(), calls=%async_computation.33 | async-start | bytes 3932160 | tf_op jit(solution)/shard_map/all_gather | solution.py:275
  754.4 333.3 %reduce-scatter.11.cloned.1.call-start = ((), (), s32[]{:S(2)}) async-start(), calls=%async_computation.16 | async-start | bytes 3932160 | tf_op jit(solution)/shard_map/reduce_scatter | solution.py:280
  798.4 23.7 %slice-start = ((s8[12582912]{0:T(1024)(128)(4,1)}), s8[4194304]{0:T(1024)(128)(4,1)S(1)}, s32[]{:S(2)}) async-start(s8[12582912]{0:T(1024)(128)(4,1)} %bitcast.845), calls=%async_computation.36 | async-start | bytes 8388608
  800.0 22.0 copy-start.149
  800.3 21.7 copy-start.172
  802.0 20.1 slice-start.1
  802.0 20.1 slice-start.2
  822.1 23.4 %slice-start.15 = ((s8[4718592]{0:T(1024)(128)(4,1)}), s8[4194304]{0:T(1024)(128)(4,1)S(1)}, s32[]{:S(2)}) async-start(s8[4718592]{0:T(1024)(128)(4,1)} %bitcast.960), calls=%async_computation.51 | async-start | bytes 8388608
  869.7 32.6 %copy-start.148 = (pred[2,1024]{1,0:T(4,128)(4,1)S(1)}, pred[2,1024]{1,0:T(4,128)(4,1)}, u32[]{:S(2)}) copy-start(pred[2,1024]{1,0:T(4,128)(4,1)} %iota_compare_fusion.2) | copy-start | bytes 6148
  942.0 208.1 %reduce-scatter.13.cloned.1.call-start = ((), (), s32[]{:S(2)}) async-start(), calls=%async_computation.17 | async-start | bytes 3932160 | tf_op jit(solution)/shard_map/reduce_scatter | solution.py:283
  955.4 302.4 %all-gather.57.cloned.1.call-start = ((), (), s32[]{:S(2)}) async-start(), calls=%async_computation.34 | async-start | bytes 3932160 | tf_op jit(solution)/shard_map/all_gather | solution.py:274
  956.0 322.7 %all-gather.59.cloned.1.call-start = ((), (), s32[]{:S(2)}) async-start(), calls=%async_computation.35 | async-start | bytes 3932160 | tf_op jit(solution)/shard_map/all_gather | solution.py:275
  958.6 381.3 %reduce-scatter.15.cloned.1.call-start = ((), (), s32[]{:S(2)}) async-start(), calls=%async_computation.18 | async-start | bytes 3932160 | tf_op jit(solution)/shard_map/reduce_scatter | solution.py:280
  959.1 201.6 %copy-start.159 = (f32[512]{0:T(512)}, f32[512]{0:T(512)S(1)}, u32[]{:S(2)}) copy-start(f32[512]{0:T(512)S(1)} %broadcast_multiply_fusion.7) | copy-start | bytes 6148
  959.4 201.3 %copy-start.161 = (f32[512]{0:T(512)}, f32[512]{0:T(512)S(1)}, u32[]{:S(2)}) copy-start(f32[512]{0:T(512)S(1)} %fusion.347) | copy-start | bytes 6148
  959.5 195.5 %copy-start.168 = (f32[512]{0:T(512)}, f32[512]{0:T(512)S(1)}, u32[]{:S(2)}) copy-start(f32[512]{0:T(512)S(1)} %broadcast_multiply_fusion.3) | copy-start | bytes 6148
  959.5 195.5 %copy-start.163 = (f32[512]{0:T(512)}, f32[512]{0:T(512)S(1)}, u32[]{:S(2)}) copy-start(f32[512]{0:T(512)S(1)} %broadcast_multiply_fusion.5) | copy-start | bytes 6148
  969.2 229.7 %copy-start.157 = (f32[512]{0:T(512)}, f32[512]{0:T(512)S(1)}, u32[]{:S(2)}) copy-start(f32[512]{0:T(512)S(1)} %fusion.348) | copy-start | bytes 6148
  975.7 111.9 %copy-start.71 = (f32[256,64]{0,1:T(8,128)S(1)}, f32[256,64]{0,1:T(8,128)}, u32[]{:S(2)}) copy-start(f32[256,64]{0,1:T(8,128)} %copy-done.69) | copy-start | bytes 196612
  1031.2 58.0 %copy-start.66 = (f32[256,64]{0,1:T(8,128)S(1)}, f32[256,64]{0,1:T(8,128)}, u32[]{:S(2)}) copy-start(f32[256,64]{0,1:T(8,128)} %copy-done.64) | copy-start | bytes 196612
  1163.6 12.7 collective-permute-start.2
  1243.1 159.3 %reduce-scatter.17.cloned.1.call-start = ((), (), s32[]{:S(2)}) async-start(), calls=%async_computation.19 | async-start | bytes 3932160 | tf_op jit(solution)/shard_map/reduce_scatter | solution.py:283
  1255.5 343.6 %reduce-scatter.19.cloned.1.call-start = ((), (), s32[]{:S(2)}) async-start(), calls=%async_computation.20 | async-start | bytes 3932160 | tf_op jit(solution)/shard_map/reduce_scatter | solution.py:280
  1261.4 155.3 %copy-start.16 = (bf16[1,2,1024,768]{2,3,1,0:T(8,128)(2,1)}, bf16[1,2,1024,768]{2,3,1,0:T(8,128)(2,1)S(1)}, u32[]{:S(2)}) copy-start(bf16[1,2,1024,768]{2,3,1,0:T(8,128)(2,1)S(1)} %copy.141) | copy-start | bytes 9437188
  1261.4 22.0 copy-start.176
  1261.4 22.0 copy-start.177
  1261.4 22.0 copy-start.106
  1283.4 129.0 %copy-start.166 = (f32[512]{0:T(512)}, f32[512]{0:T(512)S(1)}, u32[]{:S(2)}) copy-start(f32[512]{0:T(512)S(1)} %fusion.349) | copy-start | bytes 6148
  1293.5 46.5 %copy-start.72 = (f32[256,64]{0,1:T(8,128)S(1)}, f32[256,64]{0,1:T(8,128)}, u32[]{:S(2)}) copy-start(f32[256,64]{0,1:T(8,128)} %copy-done.69) | copy-start | bytes 196612
  1295.5 46.0 %copy-start.67 = (f32[256,64]{0,1:T(8,128)S(1)}, f32[256,64]{0,1:T(8,128)}, u32[]{:S(2)}) copy-start(f32[256,64]{0,1:T(8,128)} %copy-done.64) | copy-start | bytes 196612
  1415.2 12.5 collective-permute-start.3
  1427.7 19.3 slice-start.19
  1500.1 124.5 %reduce-scatter.21.cloned.1.call-start = ((), (), s32[]{:S(2)}) async-start(), calls=%async_computation.21 | async-start | bytes 3932160 | tf_op jit(solution)/shard_map/reduce_scatter | solution.py:283
  1513.2 244.6 %reduce-scatter.25.cloned.1.call-start = ((), (), s32[]{:S(2)}) async-start(), calls=%async_computation.23 | async-start | bytes 2506752 | tf_op jit(solution)/shard_map/reduce_scatter | solution.py:332
  1535.2 400.0 %reduce-scatter.27.cloned.1.call-start = ((), (), s32[]{:S(2)}) async-start(), calls=%async_computation.24 | async-start | bytes 10027008 | tf_op jit(solution)/shard_map/reduce_scatter | solution.py:333
  1554.5 557.1 %reduce-scatter.29.cloned.1.call-start = ((), (), s32[]{:S(2)}) async-start(), calls=%async_computation.25 | async-start | bytes 10027008 | tf_op jit(solution)/shard_map/reduce_scatter | solution.py:334
  1574.3 694.1 %reduce-scatter.23.cloned.1.call-start = ((), (), s32[]{:S(2)}) async-start(), calls=%async_computation.22 | async-start | bytes 7520256 | tf_op jit(solution)/shard_map/reduce_scatter | solution.py:331
  (179 other events, 922.0 us)
Sparse Core Ops, SparseCore 0:
  11.3 73.9 all-gather.40
  101.5 61.9 all-gather.30
  165.1 61.5 all-gather.28
  229.9 54.3 all-gather.42
  287.5 79.3 all-gather.44
  370.0 79.0 all-gather.46
  468.7 62.5 all-gather.34
  532.8 61.6 all-gather.32
  647.5 61.6 all-gather.38
  710.6 61.6 all-gather.36
  773.9 61.6 all-gather.48
  837.0 62.1 all-gather.50
  900.7 62.1 all-gather.52
  964.3 62.1 all-gather.54
  1028.7 58.9 reduce-scatter.10
  1089.8 60.2 reduce-scatter.12
  1151.5 63.4 all-gather.56
  1216.5 62.1 all-gather.58
  1281.0 58.9 reduce-scatter.14
  1342.1 60.2 reduce-scatter.16
  1500.2 61.1 reduce-scatter.18
  1564.2 60.2 reduce-scatter.20
  1630.0 127.7 reduce-scatter.24
  1764.8 170.3 reduce-scatter.26
  1941.5 170.1 reduce-scatter.28
  2118.2 150.1 reduce-scatter.22
where the time goes:
time: 2290 us; the launch traced here: 2280 us
  waiting for transfers between devices  1290 us (56%)
  matrix products  477 us (21%)
  local copies, waits for them, and re-layouts  204 us (9%)
  other arithmetic  188 us (8%)
  blocking collectives  86.2 us (4%)
    reduce_scatter x1, waiting for transfers between devices, local(): lax.psum_scatter(sum_in, ('dp', 'ctx'), scatter_dimension=0, tiled=True)  177 us
    reduce_scatter x1, waiting for transfers between devices, local(): lax.psum_scatter(sum_back, ('dp', 'ctx'), scatter_dimension=0, tiled=True)  176 us
    reduce_scatter x1, waiting for transfers between devices, local(): lax.psum_scatter(sum_qkv, ('dp', 'ctx'), scatter_dimension=0, tiled=True)  157 us
    reduce_scatter x3, waiting for transfers between devices, local(): lax.psum_scatter(grad_values.astype(jnp.bfloat16), 'ctx', scatter_dimensi...  142 us
    all_gather x3, waiting for transfers between devices, local(): lax.all_gather(forward_key_rows, 'ctx', axis=1, tiled=True)  109 us
    reduce_scatter x3, waiting for transfers between devices, local(): lax.psum_scatter(grad_keys.astype(jnp.bfloat16), 'ctx', scatter_dimension...  101 us
    all_gather x3, waiting for transfers between devices, local(): value_all = lax.all_gather(value_rows, 'ctx', axis=1, tiled=True)  97.5 us
    unnamed x2, blocking collectives  86.2 us
  transfers between devices with their start and end apart: 30, of which 22 were waited for; matrix products, arithmetic and copies ran while one was open for 29% of the time, Pallas kernels for 0%

commit v1 on v0

--- a/solution.py
+++ b/solution.py
@@ -173,8 +173,16 @@
             plain_rotate(query_key_value_rows[:, :, 1]).astype(jnp.bfloat16).reshape(span_shape)
         )
         forward_value_rows = query_key_value_rows[:, :, 2].astype(jnp.bfloat16).reshape(span_shape)
-        forward_key_all = lax.all_gather(forward_key_rows, "ctx", axis=1, tiled=True)
-        forward_value_all = lax.all_gather(forward_value_rows, "ctx", axis=1, tiled=True)
+        forward_key_all, forward_value_all = jnp.split(
+            lax.all_gather(
+                jnp.concatenate([forward_key_rows, forward_value_rows], axis=0),
+                "ctx",
+                axis=1,
+                tiled=True,
+            ),
+            [forward_key_rows.shape[0]],
+            axis=0,
+        )
         forward_attended_output, forward_log_total = attention_forward(
             forward_query, forward_key_all, forward_value_all, mask_for(which_batch)
         )

time: 2290 us -> 2380 us (1.039)
  waiting for transfers between devices: 1290 us -> 1380 us
    all_gather x6 -> x3, waiting for transfers between devices: 183 us -> 309 us  [local(): lax.all_gather(jnp.concatenate([forward_key_rows, forward_value_rows], ax...]
    reduce_scatter x3, waiting for transfers between devices: 101 us -> 54.4 us  [local(): lax.psum_scatter(grad_keys.astype(jnp.bfloat16), 'ctx', scatter_dimension...]
    all_gather x3, waiting for transfers between devices: 97.5 us -> 124 us  [local(): value_all = lax.all_gather(value_rows, 'ctx', axis=1, tiled=True)]
    all_gather x1, waiting for transfers between devices: 43.2 us -> 18 us  [local(): lax.all_gather(out_low, ('dp', 'ctx'), axis=0, tiled=True)]
    unnamed x439 -> x437, local copies, waits for them, and re-layouts: 59 us -> 58.5 us
  transfers between devices with their start and end apart: 30 -> 27, of which waited for: 22 -> 21; matrix products, arithmetic and copies ran while one was open for 29% -> 26% of each run, Pallas kernels for 0% -> 0%
where the time goes in v1:
time: 2380 us; the launch traced here: 2370 us
  waiting for transfers between devices  1380 us (58%)
  matrix products  471 us (20%)
  local copies, waits for them, and re-layouts  220 us (9%)
  other arithmetic  189 us (8%)
  blocking collectives  86.1 us (4%)
    all_gather x3, waiting for transfers between devices, local(): lax.all_gather(jnp.concatenate([forward_key_rows, forward_value_rows], ax...  309 us
    reduce_scatter x1, waiting for transfers between devices, local(): lax.psum_scatter(sum_in, ('dp', 'ctx'), scatter_dimension=0, tiled=True)  177 us
    reduce_scatter x1, waiting for transfers between devices, local(): lax.psum_scatter(sum_back, ('dp', 'ctx'), scatter_dimension=0, tiled=True)  177 us
    reduce_scatter x1, waiting for transfers between devices, local(): lax.psum_scatter(sum_qkv, ('dp', 'ctx'), scatter_dimension=0, tiled=True)  157 us
    reduce_scatter x3, waiting for transfers between devices, local(): lax.psum_scatter(grad_values.astype(jnp.bfloat16), 'ctx', scatter_dimensi...  140 us
    all_gather x3, waiting for transfers between devices, local(): value_all = lax.all_gather(value_rows, 'ctx', axis=1, tiled=True)  124 us
    unnamed x2, blocking collectives  86.1 us
    dot_general x12, matrix products, contract_cols(): lax.dot_general(left_op, right_op, (((1,), (1,)), ((), ())), preferred_el...  81.4 us
  transfers between devices with their start and end apart: 27, of which 21 were waited for; matrix products, arithmetic and copies ran while one was open for 26% of the time, Pallas kernels for 0%

profile of v1, /device:TPU:0, one launch (start us, length us, event | category | flops | bytes accessed | tf_op | source)
XLA Modules:
  0.0 2374.3 jit_solution(8951440777238718284)
XLA Ops:
  12.7 44.1 %all-reduce.17 = (bf16[768]{0:T(1024)(128)(2,1)S(1)}, bf16[768]{0:T(1024)(128)(2,1)S(1)}) all-reduce(bf16[768]{0:T(1024)(128)(2,1)S(1)} %dynamic-update-slice, bf16[768]{0:T(1024)(128)(2,1)S(1)} %dynamic-update-slice.1), channel_id=2, replica_groups=mesh['section'=2,'dp'=4,'ctx'=4] {'dp','ctx'}, use_global_device_ids=true, to_apply=%add.12 | all-reduce | flops 1536 | bytes 6144
  62.2 23.0 all-gather.32.cloned.1.call-done
  85.3 5.9 copy.104
  109.1 106.4 %all-gather.26.cloned.1.call-done = bf16[4,1024,768]{1,2,0:T(8,128)(2,1)} async-done(((bf16[4,256,768]{1,2,0:T(8,128)(2,1)}), bf16[4,1024,768]{1,2,0:T(8,128)(2,1)}) %all-gather.26.cloned.1.call-update) | async-done | bytes 6291472 | tf_op jit(solution)/shard_map/all_gather | solution.py:177
  219.1 11.8 select_reduce_fusion.2
  230.9 10.9 exponential_reduce_fusion.2
  241.8 11.5 broadcast_select_fusion.2
  255.2 18.0 all-gather.34.cloned.1.call-done
  276.4 79.3 %all-gather.36.cloned.1.call-done = bf16[1,768,3072]{2,1,0:T(8,128)(2,1)} async-done(((bf16[1,48,3072]{2,1,0:T(8,128)(2,1)}), bf16[1,768,3072]{2,1,0:T(8,128)(2,1)}) %all-gather.36.cloned.1.call-update) | async-done | bytes 4718608 | tf_op jit(solution)/shard_map/all_gather | solution.py:130
  359.6 21.1 bitcast_dynamic-update-slice_fusion.5
  380.8 57.3 %all-gather.38.cloned.1.call-done = bf16[1,3072,768]{2,1,0:T(8,128)(2,1)} async-done(((bf16[1,192,768]{2,1,0:T(8,128)(2,1)}), bf16[1,3072,768]{2,1,0:T(8,128)(2,1)}) %all-gather.38.cloned.1.call-update) | async-done | bytes 4718608 | tf_op jit(solution)/shard_map/all_gather | solution.py:131
  438.0 7.1 fusion.400
  479.8 91.9 %all-gather.28.cloned.1.call-done = bf16[4,1024,768]{1,2,0:T(8,128)(2,1)} async-done(((bf16[4,256,768]{1,2,0:T(8,128)(2,1)}), bf16[4,1024,768]{1,2,0:T(8,128)(2,1)}) %all-gather.28.cloned.1.call-update) | async-done | bytes 6291472 | tf_op jit(solution)/shard_map/all_gather | solution.py:177
  575.4 12.2 select_reduce_fusion.1
  587.6 10.9 exponential_reduce_fusion.1
  598.5 10.6 fusion.215
  612.6 20.4 bitcast_dynamic-update-slice_fusion.4
  723.2 6.2 bitcast_dynamic-update-slice_fusion.1
  741.5 12.4 all-gather.40.cloned.1.call-done
  758.5 14.1 fusion.406
  772.6 45.0 %all-gather.42.cloned.1.call-done = bf16[1,2,1024,768]{3,2,1,0:T(8,128)(2,1)} async-done(((bf16[1,2,256,768]{3,2,1,0:T(8,128)(2,1)}), bf16[1,2,1024,768]{3,2,1,0:T(8,128)(2,1)}) %all-gather.42.cloned.1.call-update) | async-done | bytes 3145744 | tf_op jit(solution)/shard_map/all_gather | solution.py:283
  822.3 110.5 %all-gather.30.cloned.1.call-done = bf16[4,1024,768]{1,2,0:T(8,128)(2,1)} async-done(((bf16[4,256,768]{1,2,0:T(8,128)(2,1)}), bf16[4,1024,768]{1,2,0:T(8,128)(2,1)}) %all-gather.30.cloned.1.call-update) | async-done | bytes 6291472 | tf_op jit(solution)/shard_map/all_gather | solution.py:177
  936.4 11.8 select_reduce_fusion
  948.3 11.0 exponential_reduce_fusion
  959.3 10.9 fusion.214
  979.5 19.9 bitcast_dynamic-update-slice_fusion.3
  1004.0 20.0 fusion.43
  1037.5 17.0 multiply_reduce_fusion.2
  1054.4 16.7 multiply_convert_fusion.2
  1077.7 12.8 fusion.170
  1093.0 5.0 copy.134
  1098.4 9.5 bitcast_multiply_fusion.13
  1109.9 27.1 %reduce-scatter.11.cloned.1.call-done = bf16[2,256,768]{1,2,0:T(8,128)(2,1)} async-done(((bf16[2,1024,768]{1,2,0:T(8,128)(2,1)}), bf16[2,256,768]{1,2,0:T(8,128)(2,1)}) %reduce-scatter.11.cloned.1.call-update) | async-done | bytes 786448 | tf_op jit(solution)/shard_map/reduce_scatter | solution.py:288
  1139.8 59.7 %reduce-scatter.13.cloned.1.call-done = bf16[2,256,768]{1,2,0:T(8,128)(2,1)} async-done(((bf16[2,1024,768]{1,2,0:T(8,128)(2,1)}), bf16[2,256,768]{1,2,0:T(8,128)(2,1)}) %reduce-scatter.13.cloned.1.call-update) | async-done | bytes 786448 | tf_op jit(solution)/shard_map/reduce_scatter | solution.py:291
  1214.6 10.6 fusion.407
  1225.2 39.4 %all-gather.46.cloned.1.call-done = bf16[1,2,1024,768]{3,2,1,0:T(8,128)(2,1)} async-done(((bf16[1,2,256,768]{3,2,1,0:T(8,128)(2,1)}), bf16[1,2,1024,768]{3,2,1,0:T(8,128)(2,1)}) %all-gather.46.cloned.1.call-update) | async-done | bytes 3145744 | tf_op jit(solution)/shard_map/all_gather | solution.py:283
  1270.5 18.9 fusion.48
  1296.4 18.1 multiply_reduce_fusion.1
  1314.5 16.6 multiply_convert_fusion.1
  1336.7 12.8 fusion.173
  1355.4 10.6 bitcast_multiply_fusion.11
  1368.0 27.4 %reduce-scatter.15.cloned.1.call-done = bf16[2,256,768]{1,2,0:T(8,128)(2,1)} async-done(((bf16[2,1024,768]{1,2,0:T(8,128)(2,1)}), bf16[2,256,768]{1,2,0:T(8,128)(2,1)}) %reduce-scatter.15.cloned.1.call-update) | async-done | bytes 786448 | tf_op jit(solution)/shard_map/reduce_scatter | solution.py:288
  1398.2 59.7 %reduce-scatter.17.cloned.1.call-done = bf16[2,256,768]{1,2,0:T(8,128)(2,1)} async-done(((bf16[2,1024,768]{1,2,0:T(8,128)(2,1)}), bf16[2,256,768]{1,2,0:T(8,128)(2,1)}) %reduce-scatter.17.cloned.1.call-update) | async-done | bytes 786448 | tf_op jit(solution)/shard_map/reduce_scatter | solution.py:291
  1472.4 10.6 fusion.408
  1483.0 39.8 %all-gather.50.cloned.1.call-done = bf16[1,2,1024,768]{3,2,1,0:T(8,128)(2,1)} async-done(((bf16[1,2,256,768]{3,2,1,0:T(8,128)(2,1)}), bf16[1,2,1024,768]{3,2,1,0:T(8,128)(2,1)}) %all-gather.50.cloned.1.call-update) | async-done | bytes 3145744 | tf_op jit(solution)/shard_map/all_gather | solution.py:283
  1529.9 18.2 fusion.53
  1560.6 18.2 multiply_reduce_fusion
  1578.8 16.7 multiply_convert_fusion
  1601.1 13.1 fusion.176
  1636.4 4.9 fusion.263
  1641.3 5.3 fusion.264
  1646.6 8.9 select_add_fusion.1
  1661.4 4.7 fusion.163
  1666.1 9.1 select_add_fusion
  1677.2 7.0 fusion.256
  1684.3 5.2 fusion.259
  1689.5 8.6 bitcast_multiply_fusion.9
  1702.9 20.5 reduce-scatter.21.cloned.1.call-done
  1729.7 8.6 select_add_fusion.2
  1758.7 42.0 %all-reduce.16 = (f32[768]{0:T(1024)S(1)}, f32[768]{0:T(1024)S(1)}) all-reduce(f32[768]{0:T(1024)S(1)} %select_add_fusion.5, f32[768]{0:T(1024)S(1)} %select_add_fusion.4), channel_id=24, replica_groups=mesh['section'=2,'dp'=4,'ctx'=4] {'dp','ctx'}, use_global_device_ids=true, to_apply=%region_58.59.clone | all-reduce | flops 1536 | bytes 12288
  1807.1 49.3 %reduce-scatter.25.cloned.1.call-done = f32[48,768]{1,0:T(8,128)} async-done(((f32[768,768]{1,0:T(8,128)}), f32[48,768]{1,0:T(8,128)}) %reduce-scatter.25.cloned.1.call-update) | async-done | bytes 147472 | tf_op jit(solution)/shard_map/reduce_scatter | solution.py:340
  1856.4 177.4 %reduce-scatter.27.cloned.1.call-done = f32[48,3072]{1,0:T(8,128)} async-done(((f32[768,3072]{1,0:T(8,128)}), f32[48,3072]{1,0:T(8,128)}) %reduce-scatter.27.cloned.1.call-update) | async-done | bytes 589840 | tf_op jit(solution)/shard_map/reduce_scatter | solution.py:341
  2033.8 176.7 %reduce-scatter.29.cloned.1.call-done = f32[192,768]{1,0:T(8,128)} async-done(((f32[3072,768]{1,0:T(8,128)}), f32[192,768]{1,0:T(8,128)}) %reduce-scatter.29.cloned.1.call-update) | async-done | bytes 589840 | tf_op jit(solution)/shard_map/reduce_scatter | solution.py:342
  2210.5 157.1 %reduce-scatter.23.cloned.1.call-done = f32[48,2304]{1,0:T(8,128)} async-done(((f32[768,2304]{1,0:T(8,128)}), f32[48,2304]{1,0:T(8,128)}) %reduce-scatter.23.cloned.1.call-update) | async-done | bytes 442384 | tf_op jit(solution)/shard_map/reduce_scatter | solution.py:339
  (751 shorter events, 388.2 us)
Async XLA Ops:
  7.2 78.1 %all-gather.32.cloned.1.call-start = ((), (), s32[]{:S(2)}) async-start(), calls=%async_computation.23 | async-start | bytes 3760128 | tf_op jit(solution)/shard_map/all_gather | solution.py:128
  9.0 206.5 %all-gather.26.cloned.1.call-start = ((), (), s32[]{:S(2)}) async-start(), calls=%async_computation.10 | async-start | bytes 7864320 | tf_op jit(solution)/shard_map/all_gather | solution.py:177
  56.8 602.8 %copy-start.144 = (f32[768]{0:T(1024)}, f32[768]{0:T(1024)S(1)}, u32[]{:S(2)}) copy-start(f32[768]{0:T(1024)S(1)} %convert_element_type.771) | copy-start | bytes 9220
  59.1 516.3 %copy-start.63 = (f32[256,64]{0,1:T(8,128)}, f32[256,64]{0,1:T(8,128)S(1)}, u32[]{:S(2)}) copy-start(f32[256,64]{0,1:T(8,128)S(1)} %get-tuple-element.141) | copy-start | bytes 196612
  59.1 516.3 %copy-start.68 = (f32[256,64]{0,1:T(8,128)}, f32[256,64]{0,1:T(8,128)S(1)}, u32[]{:S(2)}) copy-start(f32[256,64]{0,1:T(8,128)S(1)} %get-tuple-element.140) | copy-start | bytes 196612
  99.3 358.3 %copy-start.23 = (f32[256,12,64]{0,2,1:T(8,128)}, f32[256,12,64]{0,2,1:T(8,128)S(1)}, u32[]{:S(2)}) copy-start(f32[256,12,64]{0,2,1:T(8,128)S(1)} %mul.972) | copy-start | bytes 2359300
  99.4 355.4 %copy-start.25 = (f32[256,12,64]{0,2,1:T(8,128)}, f32[256,12,64]{0,2,1:T(8,128)S(1)}, u32[]{:S(2)}) copy-start(f32[256,12,64]{0,2,1:T(8,128)S(1)} %mul.968) | copy-start | bytes 2359300
  101.9 171.3 %all-gather.34.cloned.1.call-start = ((), (), s32[]{:S(2)}) async-start(), calls=%async_computation.24 | async-start | bytes 1253376 | tf_op jit(solution)/shard_map/all_gather | solution.py:129
  102.7 253.1 %all-gather.36.cloned.1.call-start = ((), (), s32[]{:S(2)}) async-start(), calls=%async_computation.25 | async-start | bytes 5013504 | tf_op jit(solution)/shard_map/all_gather | solution.py:130
  104.6 333.5 %all-gather.38.cloned.1.call-start = ((), (), s32[]{:S(2)}) async-start(), calls=%async_computation.26 | async-start | bytes 5013504 | tf_op jit(solution)/shard_map/all_gather | solution.py:131
  106.4 465.3 %all-gather.28.cloned.1.call-start = ((), (), s32[]{:S(2)}) async-start(), calls=%async_computation.11 | async-start | bytes 7864320 | tf_op jit(solution)/shard_map/all_gather | solution.py:177
  107.4 920.3 %copy-start.131 = (f32[768]{0:T(1024)}, f32[768]{0:T(1024)S(1)}, u32[]{:S(2)}) copy-start(f32[768]{0:T(1024)S(1)} %convert_element_type.772) | copy-start | bytes 9220
  109.1 110.0 %copy-start.79 = (f32[2,256,12,32]{1,3,2,0:T(8,128)}, f32[2,256,12,32]{1,3,2,0:T(8,128)S(1)}, u32[]{:S(2)}) copy-start(f32[2,256,12,32]{1,3,2,0:T(8,128)S(1)} %get-tuple-element.131) | copy-start | bytes 2359300
  109.1 110.0 %copy-start.80 = (f32[2,256,12,32]{1,3,2,0:T(8,128)}, f32[2,256,12,32]{1,3,2,0:T(8,128)S(1)}, u32[]{:S(2)}) copy-start(f32[2,256,12,32]{1,3,2,0:T(8,128)S(1)} %get-tuple-element.132) | copy-start | bytes 2359300
  276.1 161.9 %copy-start.33 = (f32[512,768]{1,0:T(8,128)}, f32[512,768]{1,0:T(8,128)S(1)}, u32[]{:S(2)}) copy-start(f32[512,768]{1,0:T(8,128)S(1)} %get-tuple-element.153) | copy-start | bytes 4718596
  445.2 3.4 collective-permute-start
  448.9 161.3 %copy-start.19 = (f32[2,256,768]{2,1,0:T(8,128)}, f32[2,256,768]{2,1,0:T(8,128)S(1)}, u32[]{:S(2)}) copy-start(f32[2,256,768]{2,1,0:T(8,128)S(1)} %get-tuple-element.69) | copy-start | bytes 4718596
  457.6 296.3 %all-gather.40.cloned.1.call-start = ((), (), s32[]{:S(2)}) async-start(), calls=%async_computation.27 | async-start | bytes 3932160 | tf_op jit(solution)/shard_map/all_gather | solution.py:282
  610.7 22.3 slice-start.7
  611.7 21.4 copy-start.40
  612.6 20.5 slice-start.8
  637.1 20.5 collective-permute-start.1
  692.0 125.6 %all-gather.42.cloned.1.call-start = ((), (), s32[]{:S(2)}) async-start(), calls=%async_computation.28 | async-start | bytes 3932160 | tf_op jit(solution)/shard_map/all_gather | solution.py:283
  699.4 233.3 %all-gather.30.cloned.1.call-start = ((), (), s32[]{:S(2)}) async-start(), calls=%async_computation.12 | async-start | bytes 7864320 | tf_op jit(solution)/shard_map/all_gather | solution.py:177
  703.7 389.3 %all-gather.44.cloned.1.call-start = ((), (), s32[]{:S(2)}) async-start(), calls=%async_computation.29 | async-start | bytes 3932160 | tf_op jit(solution)/shard_map/all_gather | solution.py:282
  741.0 396.0 %reduce-scatter.11.cloned.1.call-start = ((), (), s32[]{:S(2)}) async-start(), calls=%async_computation.13 | async-start | bytes 3932160 | tf_op jit(solution)/shard_map/reduce_scatter | solution.py:288
  822.3 114.1 %copy-start.64 = (f32[256,64]{0,1:T(8,128)S(1)}, f32[256,64]{0,1:T(8,128)}, u32[]{:S(2)}) copy-start(f32[256,64]{0,1:T(8,128)} %copy-done.63) | copy-start | bytes 196612
  822.3 114.1 %copy-start.69 = (f32[256,64]{0,1:T(8,128)S(1)}, f32[256,64]{0,1:T(8,128)}, u32[]{:S(2)}) copy-start(f32[256,64]{0,1:T(8,128)} %copy-done.68) | copy-start | bytes 196612
  975.8 23.6 slice-start
  977.4 21.9 copy-start.152
  977.7 21.6 copy-start.175
  999.4 24.5 %slice-start.11 = ((s8[4718592]{0:T(1024)(128)(4,1)}), s8[4194304]{0:T(1024)(128)(4,1)S(1)}, s32[]{:S(2)}) async-start(s8[4718592]{0:T(1024)(128)(4,1)} %bitcast.959), calls=%async_computation.44 | async-start | bytes 8388608
  1003.9 20.0 copy-start.4
  1003.9 20.0 copy-start.153
  1076.6 122.9 %reduce-scatter.13.cloned.1.call-start = ((), (), s32[]{:S(2)}) async-start(), calls=%async_computation.14 | async-start | bytes 3932160 | tf_op jit(solution)/shard_map/reduce_scatter | solution.py:291
  1090.5 174.1 %all-gather.46.cloned.1.call-start = ((), (), s32[]{:S(2)}) async-start(), calls=%async_computation.30 | async-start | bytes 3932160 | tf_op jit(solution)/shard_map/all_gather | solution.py:283
  1091.3 260.7 %all-gather.48.cloned.1.call-start = ((), (), s32[]{:S(2)}) async-start(), calls=%async_computation.31 | async-start | bytes 3932160 | tf_op jit(solution)/shard_map/all_gather | solution.py:282
  1092.9 302.5 %reduce-scatter.15.cloned.1.call-start = ((), (), s32[]{:S(2)}) async-start(), calls=%async_computation.15 | async-start | bytes 3932160 | tf_op jit(solution)/shard_map/reduce_scatter | solution.py:288
  1098.0 112.1 %copy-start.162 = (f32[512]{0:T(512)}, f32[512]{0:T(512)S(1)}, u32[]{:S(2)}) copy-start(f32[512]{0:T(512)S(1)} %broadcast_multiply_fusion.7) | copy-start | bytes 6148
  1098.3 111.7 %copy-start.164 = (f32[512]{0:T(512)}, f32[512]{0:T(512)S(1)}, u32[]{:S(2)}) copy-start(f32[512]{0:T(512)S(1)} %fusion.347) | copy-start | bytes 6148
  1098.3 106.0 %copy-start.171 = (f32[512]{0:T(512)}, f32[512]{0:T(512)S(1)}, u32[]{:S(2)}) copy-start(f32[512]{0:T(512)S(1)} %broadcast_multiply_fusion.3) | copy-start | bytes 6148
  1098.4 106.0 %copy-start.166 = (f32[512]{0:T(512)}, f32[512]{0:T(512)S(1)}, u32[]{:S(2)}) copy-start(f32[512]{0:T(512)S(1)} %broadcast_multiply_fusion.5) | copy-start | bytes 6148
  1107.9 29.1 %copy-start.70 = (f32[256,64]{0,1:T(8,128)S(1)}, f32[256,64]{0,1:T(8,128)}, u32[]{:S(2)}) copy-start(f32[256,64]{0,1:T(8,128)} %copy-done.68) | copy-start | bytes 196612
  1109.9 28.7 %copy-start.65 = (f32[256,64]{0,1:T(8,128)S(1)}, f32[256,64]{0,1:T(8,128)}, u32[]{:S(2)}) copy-start(f32[256,64]{0,1:T(8,128)} %copy-done.63) | copy-start | bytes 196612
  1213.3 56.0 %collective-permute-start.2 = (bf16[2,256,768]{2,1,0:T(8,128)(2,1)}, bf16[2,256,768]{2,1,0:T(8,128)(2,1)S(1)}, u32[]{:S(2)}, u32[]{:S(2)}) collective-permute-start(bf16[2,256,768]{2,1,0:T(8,128)(2,1)} %bitcast.112), channel_id=1, source_target_pairs={{16,0},{17,1},{18,2},{19,3},{20,4},{21,5},{22,6},{23,7},{24,8},{25... | collective-permute-start | bytes 2359304 | tf_op jit(solution)/shard_map/ppermute | solution.py:13
  1225.2 44.1 %copy-start.107 = (bf16[2,2,256,768]{3,2,1,0:T(8,128)(2,1)S(1)}, bf16[2,2,256,768]{3,2,1,0:T(8,128)(2,1)}, u32[]{:S(2)}) copy-start(bf16[2,2,256,768]{3,2,1,0:T(8,128)(2,1)} %param.10) | copy-start | bytes 4718596
  1269.3 23.7 copy-start.160
  1269.3 20.2 slice-start.13
  1336.7 121.2 %reduce-scatter.17.cloned.1.call-start = ((), (), s32[]{:S(2)}) async-start(), calls=%async_computation.16 | async-start | bytes 3932160 | tf_op jit(solution)/shard_map/reduce_scatter | solution.py:291
  1349.5 173.2 %all-gather.50.cloned.1.call-start = ((), (), s32[]{:S(2)}) async-start(), calls=%async_computation.32 | async-start | bytes 3932160 | tf_op jit(solution)/shard_map/all_gather | solution.py:283
  1351.9 348.2 %reduce-scatter.19.cloned.1.call-start = ((), (), s32[]{:S(2)}) async-start(), calls=%async_computation.17 | async-start | bytes 3932160 | tf_op jit(solution)/shard_map/reduce_scatter | solution.py:288
  1355.4 117.0 %copy-start.14 = (bf16[1,2,1024,768]{2,3,1,0:T(8,128)(2,1)}, bf16[1,2,1024,768]{2,3,1,0:T(8,128)(2,1)S(1)}, u32[]{:S(2)}) copy-start(bf16[1,2,1024,768]{2,3,1,0:T(8,128)(2,1)S(1)} %copy.141) | copy-start | bytes 9437188
  1355.4 112.5 %copy-start.169 = (f32[512]{0:T(512)}, f32[512]{0:T(512)S(1)}, u32[]{:S(2)}) copy-start(f32[512]{0:T(512)S(1)} %fusion.349) | copy-start | bytes 6148
  1366.0 29.4 %copy-start.71 = (f32[256,64]{0,1:T(8,128)S(1)}, f32[256,64]{0,1:T(8,128)}, u32[]{:S(2)}) copy-start(f32[256,64]{0,1:T(8,128)} %copy-done.68) | copy-start | bytes 196612
  1368.0 29.0 %copy-start.66 = (f32[256,64]{0,1:T(8,128)S(1)}, f32[256,64]{0,1:T(8,128)}, u32[]{:S(2)}) copy-start(f32[256,64]{0,1:T(8,128)} %copy-done.63) | copy-start | bytes 196612
  1471.1 56.3 %collective-permute-start.3 = (bf16[2,256,768]{2,1,0:T(8,128)(2,1)}, bf16[2,256,768]{2,1,0:T(8,128)(2,1)}, u32[]{:S(2)}, u32[]{:S(2)}) collective-permute-start(bf16[2,256,768]{2,1,0:T(8,128)(2,1)} %bitcast.136), channel_id=1, source_target_pairs={{16,0},{17,1},{18,2},{19,3},{20,4},{21,5},{22,6},{23,7},{24,8},{25... | collective-permute-start | bytes 2359304 | tf_op jit(solution)/shard_map/ppermute | solution.py:13
  1483.0 44.4 %copy-start.179 = (f32[512]{0:T(512)S(1)}, f32[512]{0:T(512)}, u32[]{:S(2)}) copy-start(f32[512]{0:T(512)} %get-tuple-element.20) | copy-start | bytes 6148
  1483.0 44.4 %copy-start.108 = (bf16[2,2,256,768]{3,2,1,0:T(8,128)(2,1)S(1)}, bf16[2,2,256,768]{3,2,1,0:T(8,128)(2,1)}, u32[]{:S(2)}) copy-start(bf16[2,2,256,768]{3,2,1,0:T(8,128)(2,1)} %param.10) | copy-start | bytes 4718596
  1527.4 20.7 slice-start.15
  1601.0 122.3 %reduce-scatter.21.cloned.1.call-start = ((), (), s32[]{:S(2)}) async-start(), calls=%async_computation.18 | async-start | bytes 3932160 | tf_op jit(solution)/shard_map/reduce_scatter | solution.py:291
  1614.2 242.2 %reduce-scatter.25.cloned.1.call-start = ((), (), s32[]{:S(2)}) async-start(), calls=%async_computation.20 | async-start | bytes 2506752 | tf_op jit(solution)/shard_map/reduce_scatter | solution.py:340
  1636.3 397.5 %reduce-scatter.27.cloned.1.call-start = ((), (), s32[]{:S(2)}) async-start(), calls=%async_computation.21 | async-start | bytes 10027008 | tf_op jit(solution)/shard_map/reduce_scatter | solution.py:341
  1655.6 554.9 %reduce-scatter.29.cloned.1.call-start = ((), (), s32[]{:S(2)}) async-start(), calls=%async_computation.22 | async-start | bytes 10027008 | tf_op jit(solution)/shard_map/reduce_scatter | solution.py:342
  1675.3 692.2 %reduce-scatter.23.cloned.1.call-start = ((), (), s32[]{:S(2)}) async-start(), calls=%async_computation.19 | async-start | bytes 7520256 | tf_op jit(solution)/shard_map/reduce_scatter | solution.py:339
  (175 other events, 836.3 us)
Sparse Core Ops, SparseCore 0:
  11.3 73.9 all-gather.31
  102.1 113.3 all-gather.25
  218.8 54.3 all-gather.33
  276.4 79.3 all-gather.35
  358.9 79.0 all-gather.37
  457.7 113.9 all-gather.27
  692.1 61.6 all-gather.39
  755.4 62.1 all-gather.41
  819.2 113.5 all-gather.29
  934.1 61.6 all-gather.43
  1076.7 60.2 reduce-scatter.10
  1139.2 60.2 reduce-scatter.12
  1201.1 63.4 all-gather.45
  1266.0 62.1 all-gather.47
  1336.8 58.5 reduce-scatter.14
  1397.6 60.2 reduce-scatter.16
  1459.3 63.4 all-gather.49
  1601.1 58.9 reduce-scatter.18
  1663.0 60.2 reduce-scatter.20
  1728.7 127.6 reduce-scatter.24
  1863.6 170.1 reduce-scatter.26
  2040.1 170.3 reduce-scatter.28
  2217.3 150.2 reduce-scatter.22
